TPU v7x, 128 devices: a whole 4x4x4 slice. The times are simulated.
128 devices in a mesh: dp: 16 (over z_lo, x, core), group: 8 (over z_hi, y).
Axes of the slice: x: 4, y: 4, z: 4 (z_hi: 2, z_lo: 2; z = z_hi * 2 + z_lo), core: 2. Of those that a mesh axis runs over, the one named last changes fastest.
Arguments:
- activations: bfloat16 [2048, 8192], P('dp'), may hold values from -6 to 6
- out_grads: bfloat16 [2048, 28672], P('dp', 'group'), may hold values from -6 to 6
- basis_in: bfloat16 [16, 512, 512], P('dp'), may hold values from -0.25 to 0.25
- basis_out: bfloat16 [56, 512, 512], P('group'), may hold values from -0.25 to 0.25
- query_grads: bfloat16 [28672, 3, 8192], P('group', None, 'dp'), may hold values from -6 to 6
- eigenvalues: bfloat16 [28672, 8192], P('group', 'dp'), may hold values from 0.049804688 to 5
- doc_ids: int32 [2048], replicated, may hold values from 0 to 63, never falling along the last dimension, each value on 1 to 64 neighbouring positions
Outputs:
- doc_scores: float32 [3, 64], replicated
Inputs may be any that keep to these rules, and one draw needn't show every extreme that they name: doc_ids never falls along the tokens; every document 0 to 63 has 1 to 64 tokens, and one has exactly 64.
All inputs are finite; a program needn't handle non-finite values.
Results may differ from a plain program's by a relative error of at most 0.0055.
Values may be sent and summed in bfloat16 or wider, within the bound.
No kernel may reach another device: no remote copies, remote signals or barrier semaphores. Data moves between devices by JAX's collectives and lax.ppermute only.
A program may use at most 192 MiB of HBM per device.

v0:
```python
import math
import jax
import jax.numpy as jnp
from jax import lax
from jax.sharding import PartitionSpec as P

D = 8192
FF = 28672
DOC_AVG = 32
damping = 0.1


def rotate_rows(rows_in, basis):
    row_count = rows_in.shape[0]
    nblocks = basis.shape[0]
    block_width = basis.shape[1]
    shaped = rows_in.reshape(row_count, nblocks, block_width)
    turned = jnp.einsum("tnb,nbc->tnc", shaped, basis, preferred_element_type=jnp.float32)
    return turned.reshape(row_count, nblocks * block_width).astype(jnp.bfloat16)


def on_device(activations, out_grads, basis_in, basis_out, query_grads, eigenvalues, doc_ids):
    blocks_in = lax.all_to_all(activations, "dp", split_axis=1, concat_axis=0, tiled=True)
    rotated_in = rotate_rows(blocks_in, basis_in)
    out_cols = query_grads.shape[0]
    queries = query_grads.shape[1]
    in_cols = query_grads.shape[2]
    scaled = (
        query_grads.astype(jnp.float32) / (eigenvalues.astype(jnp.float32)[:, None, :] + damping)
    ).astype(jnp.bfloat16)
    scaled = scaled.reshape(out_cols, queries * in_cols)
    doc_total = doc_ids.shape[0] // DOC_AVG
    doc_range = jnp.arange(doc_total, dtype=jnp.int32)
    rotated_out = rotate_rows(out_grads, basis_out)
    grad_piece = lax.all_gather(rotated_out, "dp", axis=0, tiled=True)
    piece_rows = grad_piece.shape[0]
    projected = jnp.dot(grad_piece, scaled, preferred_element_type=jnp.float32).reshape(
        piece_rows, queries, in_cols
    )
    token_scores = jnp.sum(projected * rotated_in.astype(jnp.float32)[:, None, :], axis=2)
    membership = (doc_ids[:, None] == doc_range[None, :]).astype(jnp.float32)
    local_scores = jnp.dot(
        token_scores.T,
        membership,
        precision=lax.Precision.HIGHEST,
        preferred_element_type=jnp.float32,
    )
    doc_scores = lax.psum(local_scores, ("dp", "group"))
    return doc_scores * (1.0 / math.sqrt(FF * D))


def solution(mesh):
    return jax.shard_map(
        on_device,
        mesh=mesh,
        in_specs=(
            P("dp", None),
            P("dp", "group"),
            P("dp", None, None),
            P("group", None, None),
            P("group", None, "dp"),
            P("group", "dp"),
            P(),
        ),
        out_specs=P(),
        check_vma=False,
    )
```

profile of v0, /device:TPU:1, one launch (start us, length us, event | category | flops | bytes accessed | tf_op | source)
XLA Modules:
  0.0 226.4 jit_solution(9948356858457873738)
XLA Ops:
  6.5 0.0 copy-start
  6.5 0.0 all-gather.2.cloned.1.call-start
  6.5 1.6 copy.25
  8.2 3.3 %convolution_convert_fusion.1 = bf16[7,512,128]{2,1,0:T(8,128)(2,1)S(1)} fusion(bf16[7,512,512]{2,1,0:T(8,128)(2,1)} %param.10, bf16[128,7,512]{0,2,1:T(8,128)(2,1)S(1)} %bitcast.40), kind=kOutput, calls=%fused_computation.10 | convolution fusion | flops 470220800 | bytes 5505024 | tf_op jit(solution)/shard_map/tnb,nbc->tnc/dot_general | solution.py:18
  11.5 1.3 copy.28
  12.8 0.0 all-gather.2.cloned.1.call-update
  12.8 4.1 %copy.31 = bf16[128,8192]{0,1:T(8,128)(2,1)} copy(bf16[128,8192]{1,0:T(8,128)(2,1)} %param.7) | data formatting | bytes 4194304 | tf_op args[0]
  16.9 7.2 %all-to-all-start = ((bf16[128,16,512]{0,2,1:T(8,128)(2,1)}), bf16[128,16,512]{0,2,1:T(8,128)(2,1)S(1)}, u32[]{:S(2)}, u32[]{:S(2)}) async-start(bf16[128,16,512]{0,2,1:T(8,128)(2,1)} %bitcast.38), calls=%async_computation | async-start | bytes 4194304 | tf_op jit(solution)/shard_map/all_to_all | solution.py:23
  24.1 6.4 %convert_add_fusion = f32[3584,512]{1,0:T(8,128)} fusion(bf16[3584,512]{1,0:T(8,128)(2,1)} %param.12), kind=kLoop, calls=%fused_computation.6 | loop fusion | flops 3670016 | bytes 11010048 | tf_op jit(solution)/shard_map/add | solution.py:29
  30.5 8.4 %copy.30 = f32[3584,512]{0,1:T(8,128)} copy(f32[3584,512]{1,0:T(8,128)} %convert_add_fusion) | data formatting | bytes 14680064 | tf_op jit(solution)/shard_map/add | solution.py:29
  38.9 14.7 %copy.29 = bf16[3584,3,512]{0,2,1:T(8,128)(2,1)} copy(bf16[3584,3,512]{2,0,1:T(8,128)(2,1)} %param.11) | data formatting | bytes 22020096 | tf_op args[4]
  53.6 18.2 %all-to-all-done = bf16[128,16,512]{0,2,1:T(8,128)(2,1)S(1)} async-done(((bf16[128,16,512]{0,2,1:T(8,128)(2,1)}), bf16[128,16,512]{0,2,1:T(8,128)(2,1)S(1)}, u32[]{:S(2)}, u32[]{:S(2)}) %all-to-all-start) | async-done | bytes 2097184 | tf_op jit(solution)/shard_map/all_to_all | solution.py:23
  71.8 2.6 %copy.32 = bf16[16,128,512]{2,1,0:T(8,128)(2,1)} copy(bf16[16,128,512]{1,2,0:T(8,128)(2,1)S(1)} %bitcast.37) | data formatting | bytes 4194304 | tf_op jit(solution)/shard_map/all_to_all | solution.py:23
  74.4 0.0 copy-done
  74.4 4.9 %convert_bitcast_fusion = f32[2048,512]{0,1:T(8,128)} fusion(bf16[2048,512]{1,0:T(8,128)(2,1)} %bitcast.41, bf16[1,512,512]{2,1,0:T(8,128)(2,1)S(1)} %copy-done), kind=kOutput, calls=%fused_computation.7 | convolution fusion | flops 1075838976 | bytes 6815744 | tf_op jit(solution)/shard_map/tnb,nbc->tnc/dot_general | solution.py:18
  79.4 0.0 copy-start.2
  79.4 40.7 %all-gather.2.cloned.1.call-done = bf16[2048,3584]{1,0:T(8,128)(2,1)} async-done(((bf16[128,3584]{1,0:T(8,128)(2,1)}), bf16[2048,3584]{1,0:T(8,128)(2,1)}) %all-gather.2.cloned.1.call-update) | async-done | bytes 14680080 | tf_op jit(solution)/shard_map/all_gather | solution.py:35
  120.1 0.0 copy-start.1
  120.1 31.9 %multiply_reduce_fusion = f32[2048,3]{0,1:T(4,128)S(1)} fusion(f32[2048,512]{0,1:T(8,128)} %convert_bitcast_fusion, bf16[3584,3,512]{0,2,1:T(8,128)(2,1)} %copy.29, f32[3584,512]{0,1:T(8,128)} %copy.30, bf16[2048,3584]{1,0:T(8,128)(2,1)} %all-gather.2.cloned.1.call-done), kind=kOutput, calls=%fused_computation.3 | convolution fusion | flops 22571378688 | bytes 37249024 | tf_op jit(solution)/shard_map/dot_general | solution.py:37
  152.0 0.0 copy-done.2
  152.0 0.6 fusion.10
  152.6 66.3 %psum.7 = f32[3,64]{1,0:T(4,128)S(1)} all-reduce(f32[3,64]{1,0:T(4,128)S(1)} %fusion.10), channel_id=1, replica_groups=mesh['dp'=16,'group'=8] {'dp','group'}, use_global_device_ids=true, to_apply=%region_1.0 | all-reduce | flops 192 | bytes 1536 | tf_op jit(solution)/shard_map/psum | solution.py:48
  218.9 0.6 broadcast_multiply_fusion
  219.5 0.0 copy-done.1
Async XLA Ops:
  6.5 67.9 %copy-start = (bf16[1,512,512]{2,1,0:T(8,128)(2,1)S(1)}, bf16[1,512,512]{2,1,0:T(8,128)(2,1)}, u32[]{:S(2)}) copy-start(bf16[1,512,512]{2,1,0:T(8,128)(2,1)} %param.9) | copy-start | bytes 1572868
  6.5 113.6 %all-gather.2.cloned.1.call-start = ((), (), s32[]{:S(2)}) async-start(), calls=%async_computation.1 | async-start | bytes 15597568 | tf_op jit(solution)/shard_map/all_gather | solution.py:35
  16.9 54.9 %all-to-all-start = ((bf16[128,16,512]{0,2,1:T(8,128)(2,1)}), bf16[128,16,512]{0,2,1:T(8,128)(2,1)S(1)}, u32[]{:S(2)}, u32[]{:S(2)}) async-start(bf16[128,16,512]{0,2,1:T(8,128)(2,1)} %bitcast.38), calls=%async_computation | async-start | bytes 4194304 | tf_op jit(solution)/shard_map/all_to_all | solution.py:23
  79.4 72.7 %copy-start.2 = (s32[2048]{0:T(1024)S(1)}, s32[2048]{0:T(1024)}, u32[]{:S(2)}) copy-start(s32[2048]{0:T(1024)} %param.13) | copy-start | bytes 24580
  120.1 99.4 %copy-start.1 = (bf16[1,512,512]{2,1,0:T(8,128)(2,1)S(1)}, bf16[1,512,512]{2,1,0:T(8,128)(2,1)}, u32[]{:S(2)}) copy-start(bf16[1,512,512]{2,1,0:T(8,128)(2,1)} %param.9) | copy-start | bytes 1572868
Sparse Core Ops, SparseCore 0:
  12.9 107.1 all-gather.1
where the time goes:
time: 227 us; the launch traced here: 226 us
  blocking collectives  66.3 us (29%)
  waiting for transfers between devices  58.9 us (26%)
  matrix products  40.7 us (18%)
  local copies, waits for them, and re-layouts  32.8 us (14%)
  between operations  13.4 us (6%)
  starting transfers between devices  7.16 us (3%)
  other arithmetic  6.97 us (3%)
    psum x1, blocking collectives, on_device(): doc_scores = lax.psum(local_scores, ('dp', 'group'))  66.3 us
    all_gather x1, waiting for transfers between devices, on_device(): grad_piece = lax.all_gather(rotated_out, 'dp', axis=0, tiled=True)  40.7 us
    dot_general x1, matrix products, on_device(): jnp.dot(grad_piece, scaled, preferred_element_type=jnp.float32)  31.9 us
    unnamed x9, local copies, waits for them, and re-layouts  20.4 us
    all_to_all x1, waiting for transfers between devices, on_device(): lax.all_to_all(activations, 'dp', split_axis=1, concat_axis=0, tiled=True)  18.2 us
    add x1, local copies, waits for them, and re-layouts, on_device(): eigenvalues.astype(jnp.float32)[:, None, :] + damping  8.43 us
    dot_general x2, matrix products, rotate_rows(): jnp.einsum('tnb,nbc->tnc', shaped, basis, preferred_element_type=jnp.floa...  8.25 us
    all_to_all x1, starting transfers between devices, on_device(): lax.all_to_all(activations, 'dp', split_axis=1, concat_axis=0, tiled=True)  7.16 us
  transfers between devices with their start and end apart: 2, of which 2 were waited for; matrix products, arithmetic and copies ran while one was open for 18% of the time, Pallas kernels for 0%

commit v1 on v0

--- a/solution.py
+++ b/solution.py
@@ -45,7 +45,7 @@
         precision=lax.Precision.HIGHEST,
         preferred_element_type=jnp.float32,
     )
-    doc_scores = lax.psum(local_scores, ("dp", "group"))
+    doc_scores = lax.psum(lax.psum(local_scores, "group"), "dp")
     return doc_scores * (1.0 / math.sqrt(FF * D))
 
 

time: 227 us -> 213 us (0.938)
  blocking collectives: 66.3 us -> 51.7 us
    psum x1 -> x2, blocking collectives: 66.3 us -> 51.7 us  [on_device(): doc_scores = lax.psum(lax.psum(local_scores, 'group'), 'dp')]
  transfers between devices with their start and end apart: 2 -> 2, of which waited for: 2 -> 2; matrix products, arithmetic and copies ran while one was open for 18% -> 20% of each run, Pallas kernels for 0% -> 0%
where the time goes in v1:
time: 213 us; the launch traced here: 212 us
  waiting for transfers between devices  58.8 us (28%)
  blocking collectives  51.7 us (24%)
  matrix products  40.7 us (19%)
  local copies, waits for them, and re-layouts  33 us (15%)
  between operations  13.4 us (6%)
  starting transfers between devices  7.16 us (3%)
  other arithmetic  6.98 us (3%)
    psum x2, blocking collectives, on_device(): doc_scores = lax.psum(lax.psum(local_scores, 'group'), 'dp')  51.7 us
    all_gather x1, waiting for transfers between devices, on_device(): grad_piece = lax.all_gather(rotated_out, 'dp', axis=0, tiled=True)  40.8 us
    dot_general x1, matrix products, on_device(): jnp.dot(grad_piece, scaled, preferred_element_type=jnp.float32)  31.9 us
    unnamed x9, local copies, waits for them, and re-layouts  20.7 us
    all_to_all x1, waiting for transfers between devices, on_device(): lax.all_to_all(activations, 'dp', split_axis=1, concat_axis=0, tiled=True)  18 us
    add x1, local copies, waits for them, and re-layouts, on_device(): eigenvalues.astype(jnp.float32)[:, None, :] + damping  8.38 us
    dot_general x2, matrix products, rotate_rows(): jnp.einsum('tnb,nbc->tnc', shaped, basis, preferred_element_type=jnp.floa...  8.25 us
    all_to_all x1, starting transfers between devices, on_device(): lax.all_to_all(activations, 'dp', split_axis=1, concat_axis=0, tiled=True)  7.16 us
  transfers between devices with their start and end apart: 2, of which 2 were waited for; matrix products, arithmetic and copies ran while one was open for 20% of the time, Pallas kernels for 0%

profile of v1, /device:TPU:1, one launch (start us, length us, event | category | flops | bytes accessed | tf_op | source)
XLA Modules:
  0.0 211.8 jit_solution(17007521605197737938)
XLA Ops:
  6.5 0.0 copy-start
  6.5 0.0 all-gather.2.cloned.1.call-start
  6.5 1.6 copy.25
  8.2 3.3 %convolution_convert_fusion.1 = bf16[7,512,128]{2,1,0:T(8,128)(2,1)S(1)} fusion(bf16[7,512,512]{2,1,0:T(8,128)(2,1)} %param.10, bf16[128,7,512]{0,2,1:T(8,128)(2,1)S(1)} %bitcast.40), kind=kOutput, calls=%fused_computation.10 | convolution fusion | flops 470220800 | bytes 5505024 | tf_op jit(solution)/shard_map/tnb,nbc->tnc/dot_general | solution.py:18
  11.5 1.3 copy.28
  12.8 0.0 all-gather.2.cloned.1.call-update
  12.9 4.1 %copy.31 = bf16[128,8192]{0,1:T(8,128)(2,1)} copy(bf16[128,8192]{1,0:T(8,128)(2,1)} %param.7) | data formatting | bytes 4194304 | tf_op args[0]
  16.9 7.2 %all-to-all-start = ((bf16[128,16,512]{0,2,1:T(8,128)(2,1)}), bf16[128,16,512]{0,2,1:T(8,128)(2,1)S(1)}, u32[]{:S(2)}, u32[]{:S(2)}) async-start(bf16[128,16,512]{0,2,1:T(8,128)(2,1)} %bitcast.38), calls=%async_computation | async-start | bytes 4194304 | tf_op jit(solution)/shard_map/all_to_all | solution.py:23
  24.1 6.4 %convert_add_fusion = f32[3584,512]{1,0:T(8,128)} fusion(bf16[3584,512]{1,0:T(8,128)(2,1)} %param.12), kind=kLoop, calls=%fused_computation.6 | loop fusion | flops 3670016 | bytes 11010048 | tf_op jit(solution)/shard_map/add | solution.py:29
  30.5 8.4 %copy.30 = f32[3584,512]{0,1:T(8,128)} copy(f32[3584,512]{1,0:T(8,128)} %convert_add_fusion) | data formatting | bytes 14680064 | tf_op jit(solution)/shard_map/add | solution.py:29
  38.9 15.0 %copy.29 = bf16[3584,3,512]{0,2,1:T(8,128)(2,1)} copy(bf16[3584,3,512]{2,0,1:T(8,128)(2,1)} %param.11) | data formatting | bytes 22020096 | tf_op args[4]
  53.9 18.0 %all-to-all-done = bf16[128,16,512]{0,2,1:T(8,128)(2,1)S(1)} async-done(((bf16[128,16,512]{0,2,1:T(8,128)(2,1)}), bf16[128,16,512]{0,2,1:T(8,128)(2,1)S(1)}, u32[]{:S(2)}, u32[]{:S(2)}) %all-to-all-start) | async-done | bytes 2097184 | tf_op jit(solution)/shard_map/all_to_all | solution.py:23
  71.9 2.6 %copy.32 = bf16[16,128,512]{2,1,0:T(8,128)(2,1)} copy(bf16[16,128,512]{1,2,0:T(8,128)(2,1)S(1)} %bitcast.37) | data formatting | bytes 4194304 | tf_op jit(solution)/shard_map/all_to_all | solution.py:23
  74.5 0.0 copy-done
  74.5 4.9 %convert_bitcast_fusion = f32[2048,512]{0,1:T(8,128)} fusion(bf16[2048,512]{1,0:T(8,128)(2,1)} %bitcast.41, bf16[1,512,512]{2,1,0:T(8,128)(2,1)S(1)} %copy-done), kind=kOutput, calls=%fused_computation.7 | convolution fusion | flops 1075838976 | bytes 6815744 | tf_op jit(solution)/shard_map/tnb,nbc->tnc/dot_general | solution.py:18
  79.4 0.0 copy-start.2
  79.4 40.8 %all-gather.2.cloned.1.call-done = bf16[2048,3584]{1,0:T(8,128)(2,1)} async-done(((bf16[128,3584]{1,0:T(8,128)(2,1)}), bf16[2048,3584]{1,0:T(8,128)(2,1)}) %all-gather.2.cloned.1.call-update) | async-done | bytes 14680080 | tf_op jit(solution)/shard_map/all_gather | solution.py:35
  120.1 0.0 copy-start.1
  120.1 31.9 %multiply_reduce_fusion = f32[2048,3]{0,1:T(4,128)S(1)} fusion(f32[2048,512]{0,1:T(8,128)} %convert_bitcast_fusion, bf16[3584,3,512]{0,2,1:T(8,128)(2,1)} %copy.29, f32[3584,512]{0,1:T(8,128)} %copy.30, bf16[2048,3584]{1,0:T(8,128)(2,1)} %all-gather.2.cloned.1.call-done), kind=kOutput, calls=%fused_computation.3 | convolution fusion | flops 22571378688 | bytes 37249024 | tf_op jit(solution)/shard_map/dot_general | solution.py:37
  152.1 0.0 copy-done.2
  152.1 0.6 fusion.10
  152.7 21.1 %psum.14 = f32[3,64]{1,0:T(4,128)S(1)} all-reduce(f32[3,64]{1,0:T(4,128)S(1)} %fusion.10), channel_id=1, replica_groups=mesh['dp'=16,'group'=8] {'group'}, use_global_device_ids=true, to_apply=%region_1.0 | all-reduce | flops 192 | bytes 1536 | tf_op jit(solution)/shard_map/psum | solution.py:48
  173.8 30.5 %psum.15 = f32[3,64]{1,0:T(4,128)S(1)} all-reduce(f32[3,64]{1,0:T(4,128)S(1)} %psum.14), channel_id=1, replica_groups=mesh['dp'=16,'group'=8] {'dp'}, use_global_device_ids=true, to_apply=%region_2.0 | all-reduce | flops 192 | bytes 1536 | tf_op jit(solution)/shard_map/psum | solution.py:48
  204.3 0.6 broadcast_multiply_fusion
  204.9 0.0 copy-done.1
Async XLA Ops:
  6.5 67.9 %copy-start = (bf16[1,512,512]{2,1,0:T(8,128)(2,1)S(1)}, bf16[1,512,512]{2,1,0:T(8,128)(2,1)}, u32[]{:S(2)}) copy-start(bf16[1,512,512]{2,1,0:T(8,128)(2,1)} %param.9) | copy-start | bytes 1572868
  6.5 113.6 %all-gather.2.cloned.1.call-start = ((), (), s32[]{:S(2)}) async-start(), calls=%async_computation.1 | async-start | bytes 15597568 | tf_op jit(solution)/shard_map/all_gather | solution.py:35
  16.9 54.9 %all-to-all-start = ((bf16[128,16,512]{0,2,1:T(8,128)(2,1)}), bf16[128,16,512]{0,2,1:T(8,128)(2,1)S(1)}, u32[]{:S(2)}, u32[]{:S(2)}) async-start(bf16[128,16,512]{0,2,1:T(8,128)(2,1)} %bitcast.38), calls=%async_computation | async-start | bytes 4194304 | tf_op jit(solution)/shard_map/all_to_all | solution.py:23
  79.4 72.7 %copy-start.2 = (s32[2048]{0:T(1024)S(1)}, s32[2048]{0:T(1024)}, u32[]{:S(2)}) copy-start(s32[2048]{0:T(1024)} %param.13) | copy-start | bytes 24580
  120.1 84.8 %copy-start.1 = (bf16[1,512,512]{2,1,0:T(8,128)(2,1)S(1)}, bf16[1,512,512]{2,1,0:T(8,128)(2,1)}, u32[]{:S(2)}) copy-start(bf16[1,512,512]{2,1,0:T(8,128)(2,1)} %param.9) | copy-start | bytes 1572868
Sparse Core Ops, SparseCore 0:
  13.0 107.1 all-gather.1

commit v2 on v0

--- a/solution.py
+++ b/solution.py
@@ -32,7 +32,9 @@
     doc_total = doc_ids.shape[0] // DOC_AVG
     doc_range = jnp.arange(doc_total, dtype=jnp.int32)
     rotated_out = rotate_rows(out_grads, basis_out)
-    grad_piece = lax.all_gather(rotated_out, "dp", axis=0, tiled=True)
+    grad_piece = jnp.concatenate(
+        lax.all_to_all(jnp.stack([rotated_out] * lax.axis_size("dp")), "dp", 0, 0), axis=0
+    )
     piece_rows = grad_piece.shape[0]
     projected = jnp.dot(grad_piece, scaled, preferred_element_type=jnp.float32).reshape(
         piece_rows, queries, in_cols

time: 227 us -> 350 us (1.54)
  waiting for transfers between devices: 58.9 us -> 180 us
  between operations: 13.4 us -> 0.04 us
  local copies, waits for them, and re-layouts: 32.8 us -> 40.6 us
  starting transfers between devices: 7.16 us -> 12.5 us
    all_to_all x0 -> x1, waiting for transfers between devices: none -> 159 us  [on_device(): lax.all_to_all(jnp.stack([rotated_out] * lax.axis_size('dp')), 'dp', 0, 0)]
    all_gather x1 -> x0, waiting for transfers between devices: 40.7 us -> none  [on_device(): grad_piece = lax.all_gather(rotated_out, 'dp', axis=0, tiled=True)]
    another operation x0 -> x1, local copies, waits for them, and re-layouts: none -> 7.79 us  [on_device(): jnp.stack([rotated_out] * lax.axis_size('dp'))]
    all_to_all x0 -> x1, starting transfers between devices: none -> 5.35 us  [on_device(): lax.all_to_all(jnp.stack([rotated_out] * lax.axis_size('dp')), 'dp', 0, 0)]
    unnamed x9 -> x11, local copies, waits for them, and re-layouts: 20.4 us -> 20.5 us
  transfers between devices with their start and end apart: 2 -> 2, of which waited for: 2 -> 2; matrix products, arithmetic and copies ran while one was open for 18% -> 12% of each run, Pallas kernels for 0% -> 0%
where the time goes in v2:
time: 350 us; the launch traced here: 349 us
  waiting for transfers between devices  180 us (51%)
  blocking collectives  67.6 us (19%)
  matrix products  40.9 us (12%)
  local copies, waits for them, and re-layouts  40.6 us (12%)
  starting transfers between devices  12.5 us (4%)
  other arithmetic  6.7 us (2%)
    all_to_all x1, waiting for transfers between devices, on_device(): lax.all_to_all(jnp.stack([rotated_out] * lax.axis_size('dp')), 'dp', 0, 0)  159 us
    psum x1, blocking collectives, on_device(): doc_scores = lax.psum(local_scores, ('dp', 'group'))  67.6 us
    dot_general x1, matrix products, on_device(): jnp.dot(grad_piece, scaled, preferred_element_type=jnp.float32)  31.9 us
    all_to_all x1, waiting for transfers between devices, on_device(): lax.all_to_all(activations, 'dp', split_axis=1, concat_axis=0, tiled=True)  21.4 us
    unnamed x11, local copies, waits for them, and re-layouts  20.5 us
    add x1, local copies, waits for them, and re-layouts, on_device(): eigenvalues.astype(jnp.float32)[:, None, :] + damping  8.45 us
    dot_general x2, matrix products, rotate_rows(): jnp.einsum('tnb,nbc->tnc', shaped, basis, preferred_element_type=jnp.floa...  8.41 us
    another operation x1, local copies, waits for them, and re-layouts, on_device(): jnp.stack([rotated_out] * lax.axis_size('dp'))  7.79 us
  transfers between devices with their start and end apart: 2, of which 2 were waited for; matrix products, arithmetic and copies ran while one was open for 12% of the time, Pallas kernels for 0%

profile of v2, /device:TPU:1, one launch (start us, length us, event | category | flops | bytes accessed | tf_op | source)
XLA Modules:
  0.0 348.8 jit_solution(2012826776918193946)
XLA Ops:
  0.0 0.0 copy-start
  0.0 0.0 copy-start.2
  0.0 4.2 %copy.33 = bf16[128,8192]{0,1:T(8,128)(2,1)} copy(bf16[128,8192]{1,0:T(8,128)(2,1)} %param.7) | data formatting | bytes 4194304 | tf_op args[0]
  4.2 7.2 %all-to-all-start.1 = ((bf16[128,16,512]{0,2,1:T(8,128)(2,1)}), bf16[128,16,512]{0,2,1:T(8,128)(2,1)S(1)}, u32[]{:S(2)}, u32[]{:S(2)}) async-start(bf16[128,16,512]{0,2,1:T(8,128)(2,1)} %bitcast.37), calls=%async_computation.1 | async-start | bytes 4194304 | tf_op jit(solution)/shard_map/all_to_all | solution.py:23
  11.4 0.0 copy-done.2
  11.4 1.3 copy.27
  12.7 3.6 %convolution_convert_fusion.1 = bf16[7,512,128]{2,1,0:T(8,128)(2,1)S(1)} fusion(bf16[7,512,512]{2,1,0:T(8,128)(2,1)} %param.10, bf16[128,7,512]{0,2,1:T(8,128)(2,1)} %bitcast.39), kind=kOutput, calls=%fused_computation.9 | convolution fusion | flops 470220800 | bytes 5505024 | tf_op jit(solution)/shard_map/tnb,nbc->tnc/dot_general | solution.py:18
  16.2 1.3 copy.30
  17.5 21.4 %all-to-all-done.1 = bf16[128,16,512]{0,2,1:T(8,128)(2,1)S(1)} async-done(((bf16[128,16,512]{0,2,1:T(8,128)(2,1)}), bf16[128,16,512]{0,2,1:T(8,128)(2,1)S(1)}, u32[]{:S(2)}, u32[]{:S(2)}) %all-to-all-start.1) | async-done | bytes 2097184 | tf_op jit(solution)/shard_map/all_to_all | solution.py:23
  39.0 7.8 %stack.2 = bf16[16,128,3584]{2,1,0:T(8,128)(2,1)} broadcast(bf16[128,3584]{1,0:T(8,128)(2,1)} %copy.30), dimensions={1,2} | broadcast | bytes 15597568 | tf_op jit(solution)/shard_map/stack | solution.py:36
  46.8 5.4 %all-to-all-start = ((bf16[16,128,3584]{2,1,0:T(8,128)(2,1)}), bf16[16,128,3584]{2,1,0:T(8,128)(2,1)}, u32[]{:S(2)}, u32[]{:S(2)}) async-start(bf16[16,128,3584]{2,1,0:T(8,128)(2,1)} %stack.2), calls=%async_computation | async-start | bytes 29360128 | tf_op jit(solution)/shard_map/all_to_all | solution.py:36
  52.1 6.1 %convert_add_fusion = f32[3584,512]{1,0:T(8,128)} fusion(bf16[3584,512]{1,0:T(8,128)(2,1)} %param.12), kind=kLoop, calls=%fused_computation.5 | loop fusion | flops 3670016 | bytes 11010048 | tf_op jit(solution)/shard_map/add | solution.py:29
  58.2 8.4 %copy.32 = f32[3584,512]{0,1:T(8,128)} copy(f32[3584,512]{1,0:T(8,128)} %convert_add_fusion) | data formatting | bytes 14680064 | tf_op jit(solution)/shard_map/add | solution.py:29
  66.7 15.0 %copy.31 = bf16[3584,3,512]{0,2,1:T(8,128)(2,1)} copy(bf16[3584,3,512]{2,0,1:T(8,128)(2,1)} %param.11) | data formatting | bytes 22020096 | tf_op args[4]
  81.7 2.6 copy.34
  84.2 0.0 copy-done
  84.2 4.8 %convert_bitcast_fusion = f32[2048,512]{0,1:T(8,128)} fusion(bf16[2048,512]{1,0:T(8,128)(2,1)} %bitcast.40, bf16[1,512,512]{2,1,0:T(8,128)(2,1)S(1)} %copy-done), kind=kOutput, calls=%fused_computation.6 | convolution fusion | flops 1075838976 | bytes 6815744 | tf_op jit(solution)/shard_map/tnb,nbc->tnc/dot_general | solution.py:18
  89.1 159.1 %all-to-all-done = bf16[16,128,3584]{2,1,0:T(8,128)(2,1)} async-done(((bf16[16,128,3584]{2,1,0:T(8,128)(2,1)}), bf16[16,128,3584]{2,1,0:T(8,128)(2,1)}, u32[]{:S(2)}, u32[]{:S(2)}) %all-to-all-start) | async-done | bytes 14680096 | tf_op jit(solution)/shard_map/all_to_all | solution.py:36
  248.1 0.0 copy-start.3
  248.1 0.0 copy-start.1
  248.1 31.9 %multiply_reduce_fusion = f32[2048,3]{0,1:T(4,128)S(1)} fusion(f32[2048,512]{0,1:T(8,128)} %convert_bitcast_fusion, bf16[2048,3584,1]{1,0,2:T(8,128)(2,1)} %bitcast.4, bf16[3584,3,512]{0,2,1:T(8,128)(2,1)} %copy.31, f32[3584,512]{0,1:T(8,128)} %copy.32), kind=kOutput, calls=%fused_computation.1 | convolution fusion | flops 22571378688 | bytes 37249024 | tf_op jit(solution)/shard_map/dot_general | solution.py:39
  280.1 0.0 copy-done.3
  280.1 0.6 fusion.7
  280.7 67.6 %psum.7 = f32[3,64]{1,0:T(4,128)S(1)} all-reduce(f32[3,64]{1,0:T(4,128)S(1)} %fusion.7), channel_id=1, replica_groups=mesh['dp'=16,'group'=8] {'dp','group'}, use_global_device_ids=true, to_apply=%region_1.0 | all-reduce | flops 192 | bytes 1536 | tf_op jit(solution)/shard_map/psum | solution.py:50
  348.3 0.6 broadcast_multiply_fusion
  348.8 0.0 copy-done.1
Async XLA Ops:
  0.0 84.2 %copy-start = (bf16[1,512,512]{2,1,0:T(8,128)(2,1)S(1)}, bf16[1,512,512]{2,1,0:T(8,128)(2,1)}, u32[]{:S(2)}) copy-start(bf16[1,512,512]{2,1,0:T(8,128)(2,1)} %param.9) | copy-start | bytes 1572868
  0.0 11.4 %copy-start.2 = (bf16[128,3584]{1,0:T(8,128)(2,1)S(1)}, bf16[128,3584]{1,0:T(8,128)(2,1)}, u32[]{:S(2)}) copy-start(bf16[128,3584]{1,0:T(8,128)(2,1)} %param.8) | copy-start | bytes 2752516
  4.2 34.8 %all-to-all-start.1 = ((bf16[128,16,512]{0,2,1:T(8,128)(2,1)}), bf16[128,16,512]{0,2,1:T(8,128)(2,1)S(1)}, u32[]{:S(2)}, u32[]{:S(2)}) async-start(bf16[128,16,512]{0,2,1:T(8,128)(2,1)} %bitcast.37), calls=%async_computation.1 | async-start | bytes 4194304 | tf_op jit(solution)/shard_map/all_to_all | solution.py:23
  46.8 201.4 %all-to-all-start = ((bf16[16,128,3584]{2,1,0:T(8,128)(2,1)}), bf16[16,128,3584]{2,1,0:T(8,128)(2,1)}, u32[]{:S(2)}, u32[]{:S(2)}) async-start(bf16[16,128,3584]{2,1,0:T(8,128)(2,1)} %stack.2), calls=%async_computation | async-start | bytes 29360128 | tf_op jit(solution)/shard_map/all_to_all | solution.py:36
  248.1 31.9 %copy-start.3 = (s32[2048]{0:T(1024)S(1)}, s32[2048]{0:T(1024)}, u32[]{:S(2)}) copy-start(s32[2048]{0:T(1024)} %param.13) | copy-start | bytes 24580
  248.1 100.7 %copy-start.1 = (bf16[1,512,512]{2,1,0:T(8,128)(2,1)S(1)}, bf16[1,512,512]{2,1,0:T(8,128)(2,1)}, u32[]{:S(2)}) copy-start(bf16[1,512,512]{2,1,0:T(8,128)(2,1)} %param.9) | copy-start | bytes 1572868
